TPU v7x, 512 devices: a whole 4x8x8 slice. The times are simulated.
512 devices in a mesh: head: 8 (over z), blk: 64 (over x, y, core).
Axes of the slice: x: 4, y: 8, z: 8, core: 2. Of those that a mesh axis runs over, the one named last changes fastest.
Arguments:
- vision: bfloat16 [4, 1408, 8192], P(None, 'head', 'blk'), may hold values from -600 to 600
- ln_gain: float32 [1408], P('head'), may hold values from 0.5 to 1.5
- merge_proj: bfloat16 [4, 1408, 1408], P(None, 'head'), may hold values from -0.078125 to 0.078125
- image_slot: int32 [2048], P('blk'), may hold values from 0 to 32764, as said below
- text: bfloat16 [1408, 32768], P('head', 'blk'), may hold values from -600 to 600
- rms_gain: float32 [1408], replicated, may hold values from 0.5 to 1.5
- wqkv: bfloat16 [3, 1408, 1408], P(None, 'head'), may hold values from -0.31835938 to 0.31835938
- pcache: bfloat16 [2, 1408, 131072], P(None, 'head', 'blk'), may hold values from -300 to 300
- block_table: int32 [64, 128], replicated, may hold values from -1 to 4095, as said below
- cache_len: int32 [64], P('blk'), may hold values from 1 to 4096, as said below
Outputs:
- attended: bfloat16 [1408, 32768], P('head', 'blk')
- new_cache: bfloat16 [2, 1408, 32768], P(None, 'head', 'blk')
Inputs may be any that keep to these rules, and one draw needn't show every extreme that they name: `image_slot`: pieces never intersect and start at multiples of 4; the 32 pieces held by one index of blk start in the rows of 32 different requests, and every request receives exactly 32 pieces. `block_table`: row r holds a block number for j < ceil(cache_len[r] / 32) and -1 after; no block number appears twice; index d of blk holds blocks d * 64 to (d+1) * 64 - 1. The longest request has exactly 2 blocks on every index of blk; every other request has at most one block on any index. `cache_len`: exactly one request, the longest, has 4096 cached positions; all others have fewer.
All inputs are finite; a program needn't handle non-finite values.
Results may differ from a plain program's by a relative error of at most 0.025.
The roundings to bfloat16 on the way count: a program that leaves them out, or rounds other values in their place, can miss the bound.
Values may be sent and summed in bfloat16 or wider, within the bound.
A program may use at most 128 MiB of HBM per device.

v0:
```python
import math
import jax
import jax.numpy as jnp
from jax import lax
from jax.sharding import PartitionSpec as P

D = 1408
HD = 88
BS = 32
masked_score = -1e30


def rotary_columns(values, places):
    half = values.shape[1] // 2
    freq_index = jnp.arange(half, dtype=jnp.float32)
    inverse = jnp.exp(freq_index * (-2.0 * math.log(10000.0) / values.shape[1]))
    angles = inverse[:, None] * places[None, :]
    cosine = jnp.cos(angles)[None]
    sine_part = jnp.sin(angles)[None]
    leading = values[:, :half]
    trailing = values[:, half:]
    return jnp.concatenate(
        [leading * cosine - trailing * sine_part, trailing * cosine + leading * sine_part], axis=1
    )


def softmax_part(query_block, keys, values, mask, scale):
    scores = (
        jnp.einsum("hdq,hdk->hqk", query_block, keys, preferred_element_type=jnp.float32) * scale
    )
    scores = jnp.where(mask[None], scores, masked_score)
    highest = jnp.max(scores, axis=2)
    expo = jnp.where(mask[None], jnp.exp(scores - highest[:, :, None]), 0.0)
    total = jnp.sum(expo, axis=2)
    mixed = jnp.einsum("hqk,hdk->hdq", expo, values, precision=lax.Precision.HIGHEST)
    return (mixed, highest, total)


def fold_softmax(first, second):
    mixed_a, high_a, total_a = first
    mixed_b, high_b, total_b = second
    top = jnp.maximum(high_a, high_b)
    factor_a = jnp.exp(high_a - top)
    factor_b = jnp.exp(high_b - top)
    return (
        mixed_a * factor_a[:, None, :] + mixed_b * factor_b[:, None, :],
        top,
        total_a * factor_a + total_b * factor_b,
    )


def unblock(parts):
    mixed, highest, total = parts
    heads_here = mixed.shape[1]
    mixed = jnp.transpose(mixed, (1, 2, 0, 3)).reshape(heads_here, mixed.shape[2], -1)
    highest = jnp.transpose(highest, (1, 0, 2)).reshape(heads_here, -1)
    total = jnp.transpose(total, (1, 0, 2)).reshape(heads_here, -1)
    return (mixed, highest, total)


def shards(
    vision, ln_gain, merge_proj, image_slot, text, rms_gain, wqkv, pcache, block_table, cache_len
):
    local = vision.shape[1]
    groups = vision.shape[2]
    floats = vision.astype(jnp.float32)
    totals, squares = lax.psum((jnp.sum(floats, axis=1), jnp.sum(floats * floats, axis=1)), "head")
    average = totals / D
    spread = squares / D - average * average
    normed_vision = (
        (floats - average[:, None, :])
        * lax.rsqrt(spread + 1e-06)[:, None, :]
        * ln_gain[None, :, None]
    ).astype(jnp.bfloat16)
    partial_rows = jnp.einsum(
        "tcd,tcg->dg", merge_proj, normed_vision, preferred_element_type=jnp.float32
    )
    merged_columns = lax.psum_scatter(partial_rows, "head", scatter_dimension=0, tiled=True).astype(
        jnp.bfloat16
    )
    merged = jnp.transpose(merged_columns)
    devices = lax.axis_size("blk")
    here = lax.axis_index("blk")
    rows_here = text.shape[1]
    pieces = image_slot.shape[0]
    piece_rows = groups // pieces
    lines = jnp.arange(rows_here, dtype=jnp.int32)
    offsets = jnp.arange(piece_rows, dtype=jnp.int32)
    target = image_slot // rows_here
    within = image_slot % rows_here
    select = target[None, :] == jnp.arange(devices, dtype=jnp.int32)[:, None]
    outbound = (
        jnp.dot(
            select.astype(jnp.bfloat16),
            merged.reshape(pieces, piece_rows * local),
            preferred_element_type=jnp.float32,
        )
        .astype(jnp.bfloat16)
        .reshape(devices, piece_rows, local)
    )
    starts = jnp.sum(jnp.where(select, within[None, :] + 1, 0), axis=1) - 1
    arrived, arrived_start = (
        lax.all_to_all(outbound, "blk", split_axis=0, concat_axis=0, tiled=True),
        lax.all_to_all(starts, "blk", split_axis=0, concat_axis=0, tiled=True),
    )
    row_ids = (arrived_start[:, None] + offsets[None, :]).reshape(-1)
    present = jnp.repeat(arrived_start >= 0, piece_rows)
    hits = (row_ids[:, None] == lines[None, :]) & present[:, None]
    placed_rows = jnp.einsum(
        "kl,kr->lr",
        arrived.reshape(devices * piece_rows, local),
        hits.astype(jnp.bfloat16),
        preferred_element_type=jnp.float32,
    ).astype(jnp.bfloat16)
    covered = jnp.any(hits, axis=0)
    placed = jnp.where(covered[None, :], placed_rows, text)
    row_floats = placed.astype(jnp.float32)
    square_sums = lax.psum(jnp.sum(row_floats * row_floats, axis=0), "head")
    gain_here = lax.dynamic_slice_in_dim(rms_gain, lax.axis_index("head") * local, local)
    normed = (row_floats * lax.rsqrt(square_sums / D + 1e-06)[None, :] * gain_here[:, None]).astype(
        jnp.bfloat16
    )
    projected = jnp.einsum(
        "jod,dr->jor",
        wqkv,
        lax.all_gather(normed, "head", axis=0, tiled=True),
        preferred_element_type=jnp.float32,
    )
    heads_here = local // HD
    projected = projected.reshape(3, heads_here, HD, rows_here)
    places = (cache_len[0] + lines).astype(jnp.float32)
    queries = rotary_columns(projected[0], places).astype(jnp.bfloat16)
    new_keys = rotary_columns(projected[1], places).astype(jnp.bfloat16)
    new_values = projected[2].astype(jnp.bfloat16)
    new_cache = jnp.stack(
        [new_keys.reshape(local, rows_here), new_values.reshape(local, rows_here)], axis=0
    )
    block_len = BS
    owned = pcache.shape[2] // block_len
    paged = pcache.reshape(2, local, owned, block_len)
    requests = block_table.shape[0]
    table_width = block_table.shape[1]
    slots_each = table_width // devices
    block_ids = here * owned + jnp.arange(owned, dtype=jnp.int32)
    matches = block_table[None, :, :] == block_ids[:, None, None]
    found = jnp.any(matches, axis=2)
    in_use = jnp.any(found, axis=1)
    owner = jnp.sum(jnp.where(found, jnp.arange(requests, dtype=jnp.int32)[None, :], 0), axis=1)
    logical = jnp.sum(
        jnp.where(matches, jnp.arange(table_width, dtype=jnp.int32)[None, None, :], 0), axis=(1, 2)
    )
    counter = jnp.arange(owned, dtype=jnp.int32)
    earlier = (
        (owner[:, None] == owner[None, :]) & in_use[None, :] & (counter[None, :] < counter[:, None])
    )
    standing = jnp.sum(earlier.astype(jnp.int32), axis=1)
    within_block = jnp.arange(block_len, dtype=jnp.int32)
    block_rows = min(rows_here, 512)
    count_blocks = rows_here // block_rows
    scale = HD ** (-0.5)
    query_blocks = jnp.transpose(
        queries.reshape(heads_here, HD, count_blocks, block_rows), (2, 0, 1, 3)
    )
    first_rows = jnp.arange(count_blocks, dtype=jnp.int32) * block_rows
    destination = owner * slots_each + standing
    routing = (destination[None, :] == jnp.arange(table_width, dtype=jnp.int32)[:, None]) & in_use[
        None, :
    ]
    outgoing = jnp.einsum(
        "wo,cfob->cfwb", routing.astype(jnp.bfloat16), paged, preferred_element_type=jnp.float32
    ).astype(jnp.bfloat16)
    outgoing = outgoing.reshape(2, local, table_width * block_len)
    labels = jnp.sum(jnp.where(routing, logical[None, :] + 1, 0), axis=1) - 1
    labels = labels.reshape(1, 1, table_width)
    blocks_in, labels_in = (
        lax.all_to_all(outgoing, "blk", split_axis=2, concat_axis=2, tiled=True),
        lax.all_to_all(labels, "blk", split_axis=2, concat_axis=2, tiled=True),
    )
    cached_keys = blocks_in[0].reshape(heads_here, HD, -1)
    cached_values = blocks_in[1].reshape(heads_here, HD, -1).astype(jnp.float32)
    label_flat = labels_in.reshape(-1)
    key_places = label_flat[:, None] * block_len + within_block[None, :]
    live = ((label_flat[:, None] >= 0) & (key_places < cache_len[0])).reshape(-1)
    old_mask = jnp.broadcast_to(live[None, :], (block_rows, live.shape[0]))
    new_values_f = new_values.astype(jnp.float32)

    def attend(inputs):
        query_block, first_row = inputs
        causal = (first_row + jnp.arange(block_rows, dtype=jnp.int32))[:, None] >= lines[None, :]
        old_part = softmax_part(query_block, cached_keys, cached_values, old_mask, scale)
        own_part = softmax_part(query_block, new_keys, new_values_f, causal, scale)
        return fold_softmax(old_part, own_part)

    mixed, highest, total = unblock(lax.map(attend, (query_blocks, first_rows)))
    attended = (mixed / total[:, None, :]).astype(jnp.bfloat16).reshape(local, rows_here)
    return (attended, new_cache)


def solution(mesh):
    in_specs = (
        P(None, "head", "blk"),
        P("head"),
        P(None, "head", None),
        P("blk"),
        P("head", "blk"),
        P(),
        P(None, "head", None),
        P(None, "head", "blk"),
        P(),
        P("blk"),
    )
    out_specs = (P("head", "blk"), P(None, "head", "blk"))
    return jax.shard_map(shards, mesh=mesh, in_specs=in_specs, out_specs=out_specs, check_vma=False)
```

profile of v0, /device:TPU:1, one launch (start us, length us, event | category | flops | bytes accessed | tf_op | source)
XLA Modules:
  0.0 288.2 jit_solution(1287686254156349032)
XLA Ops:
  8.3 20.3 %all-reduce = (f32[4,128]{1,0:T(4,128)S(1)}, f32[4,128]{1,0:T(4,128)S(1)}) all-reduce(f32[4,128]{1,0:T(4,128)S(1)} %get-tuple-element.23, f32[4,128]{1,0:T(4,128)S(1)} %get-tuple-element.22), channel_id=1, replica_groups=mesh['head'=8,'blk'=64] {'head'}, use_global_device_ids=true, to_apply=%region_11.12 | all-reduce | flops 1024 | bytes 8192 | tf_op jit(solution)/shard_map/psum | solution.py:67
  32.2 14.5 %all-to-all-start.2 = ((s32[64,1,1]{2,1,0:T(1,128)}), s32[64,1,1]{2,1,0:T(1,128)S(1)}, u32[]{:S(2)}, u32[]{:S(2)}) async-start(s32[64,1,1]{2,1,0:T(1,128)} %copy.44), calls=%async_computation.2 | async-start | bytes 65536 | tf_op jit(solution)/shard_map/all_to_all | solution.py:104
  46.8 2.4 compare_reduce_fusion
  51.7 3.7 %copy.38 = bf16[2,176,2048]{1,2,0:T(8,128)(2,1)} copy(bf16[2,176,2048]{2,1,0:T(8,128)(2,1)} %param.17) | data formatting | bytes 2883584 | tf_op args[7]
  55.4 13.9 %reduce-scatter.4.cloned.1.call-done = f32[176,128]{1,0:T(8,128)} async-done(((f32[1408,128]{1,0:T(8,128)}), f32[176,128]{1,0:T(8,128)}) %reduce-scatter.4.cloned.1.call-update) | async-done | bytes 90128
  70.4 14.6 %all-to-all-start.1 = ((s32[1,1,128]{1,0,2:T(1,128)}), s32[1,1,128]{1,0,2:T(1,128)S(1)}, u32[]{:S(2)}, u32[]{:S(2)}) async-start(s32[1,1,128]{1,0,2:T(1,128)} %copy.43), calls=%async_computation.1 | async-start | bytes 131072 | tf_op jit(solution)/shard_map/all_to_all | solution.py:177
  86.1 8.7 %all-to-all-done.1 = s32[1,1,128]{1,0,2:T(1,128)S(1)} async-done(((s32[1,1,128]{1,0,2:T(1,128)}), s32[1,1,128]{1,0,2:T(1,128)S(1)}, u32[]{:S(2)}, u32[]{:S(2)}) %all-to-all-start.1) | async-done | bytes 544 | tf_op jit(solution)/shard_map/all_to_all | solution.py:177
  94.8 4.4 %all-to-all-start.3 = ((bf16[64,4,176]{2,1,0:T(4,128)(2,1)}), bf16[64,4,176]{2,1,0:T(4,128)(2,1)S(1)}, u32[]{:S(2)}, u32[]{:S(2)}) async-start(bf16[64,4,176]{2,1,0:T(4,128)(2,1)} %reshape.266), calls=%async_computation.3 | async-start | bytes 262144 | tf_op jit(solution)/shard_map/all_to_all | solution.py:103
  99.2 4.9 %convert_bitcast_fusion = bf16[2,176,128,32]{2,1,3,0:T(8,128)(2,1)} fusion(bf16[2,176,64,32]{1,3,2,0:T(8,128)(2,1)} %bitcast.47, s32[64]{0:T(128)S(1)} %get-tuple-element.61, pred[64]{0:T(512)(128)(4,1)S(1)} %get-tuple-element.24), kind=kOutput, calls=%fused_computation.13 | convolution fusion | flops 186007552 | bytes 4325696 | tf_op jit(solution)/shard_map/wo,cfob->cfwb/dot_general | solution.py:169
  104.1 7.7 %copy.40 = bf16[2,176,128,32]{1,3,2,0:T(8,128)(2,1)} copy(bf16[2,176,128,32]{2,1,3,0:T(8,128)(2,1)} %convert_bitcast_fusion) | data formatting | bytes 5767168 | tf_op jit(solution)/shard_map/convert_element_type | solution.py:171
  111.8 10.1 %copy.41 = bf16[2,176,4096]{1,0,2:T(2,128)(2,1)} copy(bf16[2,176,4096]{1,2,0:T(8,128)(2,1)} %bitcast.46) | data formatting | bytes 5767168 | tf_op jit(solution)/shard_map/reshape | solution.py:172
  121.9 10.8 %all-to-all-start = ((bf16[2,176,4096]{1,0,2:T(2,128)(2,1)}), bf16[2,176,4096]{1,0,2:T(2,128)(2,1)}, u32[]{:S(2)}, u32[]{:S(2)}) async-start(bf16[2,176,4096]{1,0,2:T(2,128)(2,1)} %copy.41), calls=%async_computation | async-start | bytes 8388608 | tf_op jit(solution)/shard_map/all_to_all | solution.py:176
  135.7 13.1 %psum.23 = f32[512]{0:T(512)S(1)} all-reduce(f32[512]{0:T(512)S(1)} %get-tuple-element.55), channel_id=1, replica_groups=mesh['head'=8,'blk'=64] {'head'}, use_global_device_ids=true, to_apply=%region_14.15 | all-reduce | flops 512 | bytes 4096 | tf_op jit(solution)/shard_map/psum | solution.py:118
  150.9 2.4 multiply_reduce_fusion.1
  153.2 2.4 compare_reduce_fusion.2
  155.8 34.9 %all-gather.2.cloned.1.call-done = bf16[1408,512]{1,0:T(8,128)(2,1)} async-done(((bf16[176,512]{1,0:T(8,128)(2,1)}), bf16[1408,512]{1,0:T(8,128)(2,1)}) %all-gather.2.cloned.1.call-update) | async-done | bytes 1441808 | tf_op jit(solution)/shard_map/all_gather | solution.py:126
  190.7 2.8 fusion.15
  197.2 31.4 %all-to-all-done = bf16[2,176,4096]{1,0,2:T(2,128)(2,1)} async-done(((bf16[2,176,4096]{1,0,2:T(2,128)(2,1)}), bf16[2,176,4096]{1,0,2:T(2,128)(2,1)}, u32[]{:S(2)}, u32[]{:S(2)}) %all-to-all-start) | async-done | bytes 2883616 | tf_op jit(solution)/shard_map/all_to_all | solution.py:176
  228.6 9.8 %fusion.66 = (bf16[1,176,4096]{1,0,2:T(2,128)(2,1)}, bf16[1,176,4096]{1,0,2:T(2,128)(2,1)}) fusion(bf16[2,176,4096]{1,0,2:T(2,128)(2,1)} %all-to-all-done), kind=kLoop, calls=%fused_computation.118 | loop fusion | bytes 5767168 | tf_op jit(solution)/shard_map/slice | solution.py:180
  238.3 9.6 %copy.42 = bf16[1,176,4096]{2,1,0:T(8,128)(2,1)} copy(bf16[1,176,4096]{1,0,2:T(2,128)(2,1)} %get-tuple-element.41) | data formatting | bytes 2883584 | tf_op jit(solution)/shard_map/slice | solution.py:180
  247.9 9.8 %copy.45 = bf16[1,176,4096]{2,1,0:T(8,128)(2,1)S(1)} copy(bf16[1,176,4096]{1,0,2:T(2,128)(2,1)} %get-tuple-element.42) | data formatting | bytes 2883584 | tf_op jit(solution)/shard_map/slice | solution.py:179
  257.7 3.7 %fusion = (f32[2,512]{1,0:T(2,128)S(1)}, f32[2,512,4096]{2,1,0:T(8,128)S(1)}) fusion(pred[4096]{0:T(1024)(128)(4,1)S(1)} %and.63, bf16[2,88,4096]{2,1,0:T(8,128)(2,1)S(1)} %bitcast.48, bf16[2,44,512]{2,1,0:T(8,128)(2,1)} %copy-done.8, bf16[2,44,512]{2,1,0:T(8,128)(2,1)S(1)} %get-tuple-element.45), kind=kOutput, calls=%fused_computation.2 | convolution fusion | flops 751139840 | bytes 18407424 | tf_op jit(solution)/shard_map/while/body/eval_jaxpr/hdq,hdk->hqk/dot_general | solution.py:29
  261.5 5.1 %fusion.1 = f32[2,512]{1,0:T(2,128)S(1)} fusion(f32[2,512,4096]{2,1,0:T(8,128)S(1)} %get-tuple-element.60, f32[2,512]{1,0:T(2,128)S(1)} %get-tuple-element.59, pred[4096]{0:T(1024)(128)(4,1)S(1)} %and.63), kind=kLoop, calls=%fused_computation.3 | loop fusion | flops 20970496 | bytes 16789504 | tf_op jit(solution)/shard_map/while/body/eval_jaxpr/reduce_sum | solution.py:34
  268.1 13.2 %fusion.29 = bf16[2,88,512]{2,1,0:T(8,128)(2,1)} fusion(f32[2,88,512]{2,1,0:T(8,128)S(1)} %fusion.20, bf16[2,88,4096]{2,1,0:T(8,128)(2,1)S(1)} %bitcast.51, f32[2,512,4096]{2,1,0:T(8,128)S(1)} %get-tuple-element.60, f32[2,512]{1,0:T(2,128)S(1)} %get-tuple-element.59, pred[4096]{0:T(1024)(128)(4,1)S(1)} %and.63, f32[2,512]{1,0:T(2,128)S(1)} %get-tuple-element.28, ...), kind=kOutput, calls=%fused_computation.39 | convolution fusion | flops 4446322688 | bytes 18776064 | tf_op jit(solution)/shard_map/while/body/eval_jaxpr/hqk,hdk->hdq/dot_general | solution.py:35
  (78 shorter events, 19.1 us)
Async XLA Ops:
  7.2 21.5 %copy-start = (bf16[4,176,1408]{2,1,0:T(8,128)(2,1)S(1)}, bf16[4,176,1408]{2,1,0:T(8,128)(2,1)}, u32[]{:S(2)}) copy-start(bf16[4,176,1408]{2,1,0:T(8,128)(2,1)} %param.12) | copy-start | bytes 5947396
  7.2 62.0 %reduce-scatter.4.cloned.1.call-start = ((), (), s32[]{:S(2)}) async-start(), calls=%async_computation.6 | async-start | bytes 811008
  28.6 2.7 copy-start.11
  28.6 18.1 %copy-start.9 = (s32[64,128]{1,0:T(8,128)S(1)}, s32[64,128]{1,0:T(8,128)}, u32[]{:S(2)}) copy-start(s32[64,128]{1,0:T(8,128)} %param.18) | copy-start | bytes 98308
  32.2 38.2 %all-to-all-start.2 = ((s32[64,1,1]{2,1,0:T(1,128)}), s32[64,1,1]{2,1,0:T(1,128)S(1)}, u32[]{:S(2)}, u32[]{:S(2)}) async-start(s32[64,1,1]{2,1,0:T(1,128)} %copy.44), calls=%async_computation.2 | async-start | bytes 65536 | tf_op jit(solution)/shard_map/all_to_all | solution.py:104
  70.4 24.4 %all-to-all-start.1 = ((s32[1,1,128]{1,0,2:T(1,128)}), s32[1,1,128]{1,0,2:T(1,128)S(1)}, u32[]{:S(2)}, u32[]{:S(2)}) async-start(s32[1,1,128]{1,0,2:T(1,128)} %copy.43), calls=%async_computation.1 | async-start | bytes 131072 | tf_op jit(solution)/shard_map/all_to_all | solution.py:177
  94.8 27.1 %all-to-all-start.3 = ((bf16[64,4,176]{2,1,0:T(4,128)(2,1)}), bf16[64,4,176]{2,1,0:T(4,128)(2,1)S(1)}, u32[]{:S(2)}, u32[]{:S(2)}) async-start(bf16[64,4,176]{2,1,0:T(4,128)(2,1)} %reshape.266), calls=%async_computation.3 | async-start | bytes 262144 | tf_op jit(solution)/shard_map/all_to_all | solution.py:103
  121.9 13.5 %copy-start.10 = (bf16[176,512]{1,0:T(8,128)(2,1)S(1)}, bf16[176,512]{1,0:T(8,128)(2,1)}, u32[]{:S(2)}) copy-start(bf16[176,512]{1,0:T(8,128)(2,1)} %param.14) | copy-start | bytes 540676
  121.9 106.7 %all-to-all-start = ((bf16[2,176,4096]{1,0,2:T(2,128)(2,1)}), bf16[2,176,4096]{1,0,2:T(2,128)(2,1)}, u32[]{:S(2)}, u32[]{:S(2)}) async-start(bf16[2,176,4096]{1,0,2:T(2,128)(2,1)} %copy.41), calls=%async_computation | async-start | bytes 8388608 | tf_op jit(solution)/shard_map/all_to_all | solution.py:176
  132.7 58.0 %all-gather.2.cloned.1.call-start = ((), (), s32[]{:S(2)}) async-start(), calls=%async_computation.5 | async-start | bytes 1622016 | tf_op jit(solution)/shard_map/all_gather | solution.py:126
  150.5 44.8 %copy-start.4 = (pred[512,512]{0,1:T(8,128)(4,1)}, pred[512,512]{0,1:T(8,128)(4,1)S(1)}, u32[]{:S(2)}) copy-start(pred[512,512]{0,1:T(8,128)(4,1)S(1)} %iota_compare_fusion) | copy-start | bytes 786436
  193.6 1.0 copy-start.6
  194.6 2.6 copy-start.8
  195.2 1.4 copy-start.1
  261.4 5.2 %copy-start.2 = (f32[2,512,512]{1,2,0:T(8,128)S(1)}, f32[2,512,512]{1,2,0:T(8,128)}, u32[]{:S(2)}) copy-start(f32[2,512,512]{1,2,0:T(8,128)} %copy-done.1) | copy-start | bytes 6291460
  261.5 5.2 %copy-start.5 = (pred[512,512]{0,1:T(8,128)(4,1)S(1)}, pred[512,512]{0,1:T(8,128)(4,1)}, u32[]{:S(2)}) copy-start(pred[512,512]{0,1:T(8,128)(4,1)} %copy-done.4) | copy-start | bytes 786436
  261.5 5.2 %copy-start.7 = (bf16[1,176,512]{2,1,0:T(8,128)(2,1)S(1)}, bf16[1,176,512]{2,1,0:T(8,128)(2,1)}, u32[]{:S(2)}) copy-start(bf16[1,176,512]{2,1,0:T(8,128)(2,1)} %copy-done.6) | copy-start | bytes 540676
  266.6 1.5 copy-start.3
Sparse Core Ops, SparseCore 0:
  31.5 37.7 reduce-scatter.3
  149.8 40.8 all-gather.1
where the time goes:
time: 290 us; the launch traced here: 288 us
  waiting for transfers between devices  88.9 us (31%)
  local copies, waits for them, and re-layouts  57.9 us (20%)
  starting transfers between devices  44.4 us (15%)
  blocking collectives  33.4 us (12%)
  matrix products  28.9 us (10%)
  other arithmetic  19.6 us (7%)
  between operations  15.1 us (5%)
    all_gather x1, waiting for transfers between devices, shards(): lax.all_gather(normed, 'head', axis=0, tiled=True)  34.9 us
    all_to_all x1, waiting for transfers between devices, shards(): lax.all_to_all(outgoing, 'blk', split_axis=2, concat_axis=2, tiled=True)  31.4 us
    psum x1, blocking collectives, shards(): lax.psum((jnp.sum(floats, axis=1), jnp.sum(floats * floats, axis=1)), 'he...  20.3 us
    slice x2, local copies, waits for them, and re-layouts, shards(): cached_values = blocks_in[1].reshape(heads_here, HD, -1).astype(jnp.float32)  19.4 us
    dot_general x2, matrix products, softmax_part(): jnp.einsum('hqk,hdk->hdq', expo, values, precision=lax.Precision.HIGHEST)  14.7 us
    all_to_all x1, starting transfers between devices, shards(): lax.all_to_all(labels, 'blk', split_axis=2, concat_axis=2, tiled=True)  14.6 us
    all_to_all x1, starting transfers between devices, shards(): lax.all_to_all(starts, 'blk', split_axis=0, concat_axis=0, tiled=True)  14.5 us
    unnamed x3, waiting for transfers between devices  13.9 us
  transfers between devices with their start and end apart: 6, of which 4 were waited for; matrix products, arithmetic and copies ran while one was open for 17% of the time, Pallas kernels for 0%

commit v1 on v0

--- a/solution.py
+++ b/solution.py
@@ -120,11 +120,26 @@
     normed = (row_floats * lax.rsqrt(square_sums / D + 1e-06)[None, :] * gain_here[:, None]).astype(
         jnp.bfloat16
     )
+
+    def _wait_rails(sample, comm_axis, d_out):
+        count_all = lax.axis_size(comm_axis)
+        rack = [(q, (q + 1) % count_all) for q in range(count_all)]
+        fields = [(q, (q - 1) % count_all) for q in range(count_all)]
+        value_now, piece_now = ([sample], [sample])
+        for _ in range(count_all // 2):
+            value_now.append(lax.ppermute(value_now[-1], comm_axis, rack))
+        c = 0
+        while c < (count_all - 1) // 2:
+            piece_now.append(lax.ppermute(piece_now[-1], comm_axis, fields))
+            c = c + 1
+        n_now = jnp.concatenate([*value_now[::-1], *piece_now[1:]], axis=d_out)
+        u_next = jnp.roll(
+            n_now, (lax.axis_index(comm_axis) - count_all // 2) * sample.shape[d_out], axis=d_out
+        )
+        return u_next
+
     projected = jnp.einsum(
-        "jod,dr->jor",
-        wqkv,
-        lax.all_gather(normed, "head", axis=0, tiled=True),
-        preferred_element_type=jnp.float32,
+        "jod,dr->jor", wqkv, _wait_rails(normed, "head", 0), preferred_element_type=jnp.float32
     )
     heads_here = local // HD
     projected = projected.reshape(3, heads_here, HD, rows_here)

time: 290 us -> 278 us (0.959)
  waiting for transfers between devices: 88.9 us -> 61.1 us
  starting transfers between devices: 44.4 us -> 59.2 us
  local copies, waits for them, and re-layouts: 57.9 us -> 61.9 us
    all_gather x1 -> x0, waiting for transfers between devices: 34.9 us -> none  [shards(): lax.all_gather(normed, 'head', axis=0, tiled=True)]
    ppermute x0 -> x7, starting transfers between devices: none -> 23.7 us  [the longest x3 14.3 us: _wait_rails(): piece_now.append(lax.ppermute(piece_now[-1], comm_axis, fields))]
    unnamed x3 -> x2, waiting for transfers between devices: 13.9 us -> 0.04 us
    all_to_all x1, waiting for transfers between devices: 0.01 us -> 10.3 us  [shards(): lax.all_to_all(outbound, 'blk', split_axis=0, concat_axis=0, tiled=True)]
    all_to_all x1, waiting for transfers between devices: 31.4 us -> 38.9 us  [shards(): lax.all_to_all(outgoing, 'blk', split_axis=2, concat_axis=2, tiled=True)]
    ppermute x0 -> x7, waiting for transfers between devices: none -> 5.8 us  [the longest x4 5.52 us: _wait_rails(): value_now.append(lax.ppermute(value_now[-1], comm_axis, rack))]
    all_to_all x1, starting transfers between devices: 10.8 us -> 5.43 us  [shards(): lax.all_to_all(outgoing, 'blk', split_axis=2, concat_axis=2, tiled=True)]
    unnamed x27 -> x40, local copies, waits for them, and re-layouts: 7.2 us -> 11.2 us
  transfers between devices with their start and end apart: 6 -> 12, of which waited for: 4 -> 7; matrix products, arithmetic and copies ran while one was open for 17% -> 19% of each run, Pallas kernels for 0% -> 0%
where the time goes in v1:
time: 278 us; the launch traced here: 276 us
  local copies, waits for them, and re-layouts  61.9 us (22%)
  waiting for transfers between devices  61.1 us (22%)
  starting transfers between devices  59.2 us (21%)
  blocking collectives  32 us (12%)
  matrix products  27.1 us (10%)
  other arithmetic  19.6 us (7%)
  between operations  15.3 us (6%)
    all_to_all x1, waiting for transfers between devices, shards(): lax.all_to_all(outgoing, 'blk', split_axis=2, concat_axis=2, tiled=True)  38.9 us
    psum x1, blocking collectives, shards(): lax.psum((jnp.sum(floats, axis=1), jnp.sum(floats * floats, axis=1)), 'he...  19.7 us
    slice x2, local copies, waits for them, and re-layouts, shards(): cached_values = blocks_in[1].reshape(heads_here, HD, -1).astype(jnp.float32)  19.4 us
    dot_general x2, matrix products, softmax_part(): jnp.einsum('hqk,hdk->hdq', expo, values, precision=lax.Precision.HIGHEST)  14.7 us
    ppermute x3, starting transfers between devices, _wait_rails(): piece_now.append(lax.ppermute(piece_now[-1], comm_axis, fields))  14.3 us
    all_to_all x1, starting transfers between devices, shards(): lax.all_to_all(labels, 'blk', split_axis=2, concat_axis=2, tiled=True)  13.8 us
    psum x1, blocking collectives, shards(): square_sums = lax.psum(jnp.sum(row_floats * row_floats, axis=0), 'head')  12.3 us
    all_to_all x1, starting transfers between devices, shards(): lax.all_to_all(starts, 'blk', split_axis=0, concat_axis=0, tiled=True)  11.6 us
  transfers between devices with their start and end apart: 12, of which 7 were waited for; matrix products, arithmetic and copies ran while one was open for 19% of the time, Pallas kernels for 0%

profile of v1, /device:TPU:1, one launch (start us, length us, event | category | flops | bytes accessed | tf_op | source)
XLA Modules:
  0.0 276.1 jit_solution(3973189513514807957)
XLA Ops:
  8.8 11.6 %all-to-all-start.2 = ((s32[64,1,1]{2,1,0:T(1,128)}), s32[64,1,1]{2,1,0:T(1,128)S(1)}, u32[]{:S(2)}, u32[]{:S(2)}) async-start(s32[64,1,1]{2,1,0:T(1,128)} %copy.44), calls=%async_computation.2 | async-start | bytes 65536 | tf_op jit(solution)/shard_map/all_to_all | solution.py:104
  21.5 19.7 %all-reduce = (f32[4,128]{1,0:T(4,128)S(1)}, f32[4,128]{1,0:T(4,128)S(1)}) all-reduce(f32[4,128]{1,0:T(4,128)S(1)} %get-tuple-element.23, f32[4,128]{1,0:T(4,128)S(1)} %get-tuple-element.22), channel_id=1, replica_groups=mesh['head'=8,'blk'=64] {'head'}, use_global_device_ids=true, to_apply=%region_11.12 | all-reduce | flops 1024 | bytes 8192 | tf_op jit(solution)/shard_map/psum | solution.py:67
  47.1 3.7 %copy.38 = bf16[2,176,2048]{1,2,0:T(8,128)(2,1)} copy(bf16[2,176,2048]{2,1,0:T(8,128)(2,1)} %param.17) | data formatting | bytes 2883584 | tf_op args[7]
  52.5 4.9 %convert_bitcast_fusion = bf16[2,176,128,32]{2,1,3,0:T(8,128)(2,1)} fusion(bf16[2,176,64,32]{1,3,2,0:T(8,128)(2,1)} %bitcast.47, s32[64]{0:T(128)S(1)} %get-tuple-element.61, pred[64]{0:T(512)(128)(4,1)S(1)} %get-tuple-element.24), kind=kOutput, calls=%fused_computation.13 | convolution fusion | flops 186007552 | bytes 4325696 | tf_op jit(solution)/shard_map/wo,cfob->cfwb/dot_general | solution.py:184
  58.1 7.7 %copy.40 = bf16[2,176,128,32]{1,3,2,0:T(8,128)(2,1)} copy(bf16[2,176,128,32]{2,1,3,0:T(8,128)(2,1)} %convert_bitcast_fusion) | data formatting | bytes 5767168 | tf_op jit(solution)/shard_map/convert_element_type | solution.py:186
  65.8 10.1 %copy.41 = bf16[2,176,4096]{1,0,2:T(2,128)(2,1)} copy(bf16[2,176,4096]{1,2,0:T(8,128)(2,1)} %bitcast.46) | data formatting | bytes 5767168 | tf_op jit(solution)/shard_map/reshape | solution.py:187
  76.7 13.8 %all-to-all-start.1 = ((s32[1,1,128]{1,0,2:T(1,128)}), s32[1,1,128]{1,0,2:T(1,128)S(1)}, u32[]{:S(2)}, u32[]{:S(2)}) async-start(s32[1,1,128]{1,0,2:T(1,128)} %copy.43), calls=%async_computation.1 | async-start | bytes 131072 | tf_op jit(solution)/shard_map/all_to_all | solution.py:192
  94.1 6.1 %all-to-all-done.1 = s32[1,1,128]{1,0,2:T(1,128)S(1)} async-done(((s32[1,1,128]{1,0,2:T(1,128)}), s32[1,1,128]{1,0,2:T(1,128)S(1)}, u32[]{:S(2)}, u32[]{:S(2)}) %all-to-all-start.1) | async-done | bytes 544 | tf_op jit(solution)/shard_map/all_to_all | solution.py:192
  100.2 4.6 %all-to-all-start.3 = ((bf16[64,4,176]{2,1,0:T(4,128)(2,1)}), bf16[64,4,176]{2,1,0:T(4,128)(2,1)S(1)}, u32[]{:S(2)}, u32[]{:S(2)}) async-start(bf16[64,4,176]{2,1,0:T(4,128)(2,1)} %reshape.266), calls=%async_computation.3 | async-start | bytes 262144 | tf_op jit(solution)/shard_map/all_to_all | solution.py:103
  105.1 10.3 %all-to-all-done.3 = bf16[64,4,176]{2,1,0:T(4,128)(2,1)S(1)} async-done(((bf16[64,4,176]{2,1,0:T(4,128)(2,1)}), bf16[64,4,176]{2,1,0:T(4,128)(2,1)S(1)}, u32[]{:S(2)}, u32[]{:S(2)}) %all-to-all-start.3) | async-done | bytes 90144 | tf_op jit(solution)/shard_map/all_to_all | solution.py:103
  115.3 5.4 %all-to-all-start = ((bf16[2,176,4096]{1,0,2:T(2,128)(2,1)}), bf16[2,176,4096]{1,0,2:T(2,128)(2,1)}, u32[]{:S(2)}, u32[]{:S(2)}) async-start(bf16[2,176,4096]{1,0,2:T(2,128)(2,1)} %copy.41), calls=%async_computation | async-start | bytes 8388608 | tf_op jit(solution)/shard_map/all_to_all | solution.py:191
  121.4 12.3 %psum.23 = f32[512]{0:T(512)S(1)} all-reduce(f32[512]{0:T(512)S(1)} %get-tuple-element.55), channel_id=1, replica_groups=mesh['head'=8,'blk'=64] {'head'}, use_global_device_ids=true, to_apply=%region_14.15 | all-reduce | flops 512 | bytes 4096 | tf_op jit(solution)/shard_map/psum | solution.py:118
  133.8 3.4 %collective-permute-start = (bf16[176,512]{1,0:T(8,128)(2,1)S(1)}, bf16[176,512]{1,0:T(8,128)(2,1)S(1)}, u32[]{:S(2)}, u32[]{:S(2)}) collective-permute-start(bf16[176,512]{1,0:T(8,128)(2,1)S(1)} %multiply_convert_fusion), channel_id=1, source_target_pairs={{0,64},{64,128},{128,192},{192,256},{256,320},{320,384},{384,448},... | collective-permute-start | bytes 540680 | tf_op jit(solution)/shard_map/ppermute | solution.py:130
  137.3 4.4 %collective-permute-done = bf16[176,512]{1,0:T(8,128)(2,1)S(1)} collective-permute-done((bf16[176,512]{1,0:T(8,128)(2,1)S(1)}, bf16[176,512]{1,0:T(8,128)(2,1)S(1)}, u32[]{:S(2)}, u32[]{:S(2)}) %collective-permute-start) | collective-permute-done | bytes 180256 | tf_op jit(solution)/shard_map/ppermute | solution.py:130
  144.2 4.3 %collective-permute-start.4 = (bf16[176,512]{1,0:T(8,128)(2,1)S(1)}, bf16[176,512]{1,0:T(8,128)(2,1)S(1)}, u32[]{:S(2)}, u32[]{:S(2)}) collective-permute-start(bf16[176,512]{1,0:T(8,128)(2,1)S(1)} %multiply_convert_fusion), channel_id=1, source_target_pairs={{0,448},{64,0},{128,64},{192,128},{256,192},{320,256},{384,320},{4... | collective-permute-start | bytes 540680 | tf_op jit(solution)/shard_map/ppermute | solution.py:133
  156.1 4.6 %collective-permute-start.5 = (bf16[176,512]{1,0:T(8,128)(2,1)S(1)}, bf16[176,512]{1,0:T(8,128)(2,1)S(1)}, u32[]{:S(2)}, u32[]{:S(2)}) collective-permute-start(bf16[176,512]{1,0:T(8,128)(2,1)S(1)} %collective-permute-done.4), channel_id=1, source_target_pairs={{0,448},{64,0},{128,64},{192,128},{256,192},{320,256},{384,320},{4... | collective-permute-start | bytes 540680 | tf_op jit(solution)/shard_map/ppermute | solution.py:133
  163.1 5.4 %collective-permute-start.6 = (bf16[176,512]{1,0:T(8,128)(2,1)S(1)}, bf16[176,512]{1,0:T(8,128)(2,1)S(1)}, u32[]{:S(2)}, u32[]{:S(2)}) collective-permute-start(bf16[176,512]{1,0:T(8,128)(2,1)S(1)} %collective-permute-done.5), channel_id=1, source_target_pairs={{0,448},{64,0},{128,64},{192,128},{256,192},{320,256},{384,320},{4... | collective-permute-start | bytes 540680 | tf_op jit(solution)/shard_map/ppermute | solution.py:133
  177.8 38.9 %all-to-all-done = bf16[2,176,4096]{1,0,2:T(2,128)(2,1)} async-done(((bf16[2,176,4096]{1,0,2:T(2,128)(2,1)}), bf16[2,176,4096]{1,0,2:T(2,128)(2,1)}, u32[]{:S(2)}, u32[]{:S(2)}) %all-to-all-start) | async-done | bytes 2883616 | tf_op jit(solution)/shard_map/all_to_all | solution.py:191
  216.7 9.8 %fusion.68 = (bf16[1,176,4096]{1,0,2:T(2,128)(2,1)}, bf16[1,176,4096]{1,0,2:T(2,128)(2,1)}) fusion(bf16[2,176,4096]{1,0,2:T(2,128)(2,1)} %all-to-all-done), kind=kLoop, calls=%fused_computation.136 | loop fusion | bytes 5767168 | tf_op jit(solution)/shard_map/slice | solution.py:195
  226.5 9.6 %copy.42 = bf16[1,176,4096]{2,1,0:T(8,128)(2,1)} copy(bf16[1,176,4096]{1,0,2:T(2,128)(2,1)} %get-tuple-element.41) | data formatting | bytes 2883584 | tf_op jit(solution)/shard_map/slice | solution.py:195
  236.1 9.8 %copy.45 = bf16[1,176,4096]{2,1,0:T(8,128)(2,1)S(1)} copy(bf16[1,176,4096]{1,0,2:T(2,128)(2,1)} %get-tuple-element.42) | data formatting | bytes 2883584 | tf_op jit(solution)/shard_map/slice | solution.py:194
  245.9 3.7 %fusion = (f32[2,512]{1,0:T(2,128)S(1)}, f32[2,512,4096]{2,1,0:T(8,128)S(1)}) fusion(pred[4096]{0:T(1024)(128)(4,1)S(1)} %and.68, bf16[2,88,4096]{2,1,0:T(8,128)(2,1)S(1)} %bitcast.48, bf16[2,44,512]{2,1,0:T(8,128)(2,1)} %copy-done.8, bf16[2,44,512]{2,1,0:T(8,128)(2,1)S(1)} %get-tuple-element.45), kind=kOutput, calls=%fused_computation.2 | convolution fusion | flops 751139840 | bytes 18407424 | tf_op jit(solution)/shard_map/while/body/eval_jaxpr/hdq,hdk->hqk/dot_general | solution.py:29
  249.6 4.9 %fusion.1 = f32[2,512]{1,0:T(2,128)S(1)} fusion(f32[2,512,4096]{2,1,0:T(8,128)S(1)} %get-tuple-element.60, f32[2,512]{1,0:T(2,128)S(1)} %get-tuple-element.59, pred[4096]{0:T(1024)(128)(4,1)S(1)} %and.68), kind=kLoop, calls=%fused_computation.3 | loop fusion | flops 20970496 | bytes 16789504 | tf_op jit(solution)/shard_map/while/body/eval_jaxpr/reduce_sum | solution.py:34
  256.1 13.2 %fusion.30 = bf16[2,88,512]{2,1,0:T(8,128)(2,1)} fusion(f32[2,88,512]{2,1,0:T(8,128)S(1)} %fusion.21, bf16[2,88,4096]{2,1,0:T(8,128)(2,1)S(1)} %bitcast.51, f32[2,512,4096]{2,1,0:T(8,128)S(1)} %get-tuple-element.60, f32[2,512]{1,0:T(2,128)S(1)} %get-tuple-element.59, pred[4096]{0:T(1024)(128)(4,1)S(1)} %and.68, f32[2,512]{1,0:T(2,128)S(1)} %get-tuple-element.28, ...), kind=kOutput, calls=%fused_computation.40 | convolution fusion | flops 4446322688 | bytes 18776064 | tf_op jit(solution)/shard_map/while/body/eval_jaxpr/hqk,hdk->hdq/dot_general | solution.py:35
  (105 shorter events, 38.7 us)
Async XLA Ops:
  7.2 34.0 %copy-start = (bf16[4,176,1408]{2,1,0:T(8,128)(2,1)S(1)}, bf16[4,176,1408]{2,1,0:T(8,128)(2,1)}, u32[]{:S(2)}) copy-start(bf16[4,176,1408]{2,1,0:T(8,128)(2,1)} %param.12) | copy-start | bytes 5947396
  7.2 37.4 %copy-start.9 = (s32[64,128]{1,0:T(8,128)S(1)}, s32[64,128]{1,0:T(8,128)}, u32[]{:S(2)}) copy-start(s32[64,128]{1,0:T(8,128)} %param.18) | copy-start | bytes 98308
  8.8 67.9 %all-to-all-start.2 = ((s32[64,1,1]{2,1,0:T(1,128)}), s32[64,1,1]{2,1,0:T(1,128)S(1)}, u32[]{:S(2)}, u32[]{:S(2)}) async-start(s32[64,1,1]{2,1,0:T(1,128)} %copy.44), calls=%async_computation.2 | async-start | bytes 65536 | tf_op jit(solution)/shard_map/all_to_all | solution.py:104
  20.4 71.5 %reduce-scatter.4.cloned.1.call-start = ((), (), s32[]{:S(2)}) async-start(), calls=%async_computation.5 | async-start | bytes 811008
  76.7 23.6 %all-to-all-start.1 = ((s32[1,1,128]{1,0,2:T(1,128)}), s32[1,1,128]{1,0,2:T(1,128)S(1)}, u32[]{:S(2)}, u32[]{:S(2)}) async-start(s32[1,1,128]{1,0,2:T(1,128)} %copy.43), calls=%async_computation.1 | async-start | bytes 131072 | tf_op jit(solution)/shard_map/all_to_all | solution.py:192
  100.2 15.1 %all-to-all-start.3 = ((bf16[64,4,176]{2,1,0:T(4,128)(2,1)}), bf16[64,4,176]{2,1,0:T(4,128)(2,1)S(1)}, u32[]{:S(2)}, u32[]{:S(2)}) async-start(bf16[64,4,176]{2,1,0:T(4,128)(2,1)} %reshape.266), calls=%async_computation.3 | async-start | bytes 262144 | tf_op jit(solution)/shard_map/all_to_all | solution.py:103
  105.1 16.0 %copy-start.11 = (bf16[176,512]{1,0:T(8,128)(2,1)S(1)}, bf16[176,512]{1,0:T(8,128)(2,1)}, u32[]{:S(2)}) copy-start(bf16[176,512]{1,0:T(8,128)(2,1)} %param.14) | copy-start | bytes 540676
  115.3 101.4 %all-to-all-start = ((bf16[2,176,4096]{1,0,2:T(2,128)(2,1)}), bf16[2,176,4096]{1,0,2:T(2,128)(2,1)}, u32[]{:S(2)}, u32[]{:S(2)}) async-start(bf16[2,176,4096]{1,0,2:T(2,128)(2,1)} %copy.41), calls=%async_computation | async-start | bytes 8388608 | tf_op jit(solution)/shard_map/all_to_all | solution.py:191
  133.8 7.8 %collective-permute-start = (bf16[176,512]{1,0:T(8,128)(2,1)S(1)}, bf16[176,512]{1,0:T(8,128)(2,1)S(1)}, u32[]{:S(2)}, u32[]{:S(2)}) collective-permute-start(bf16[176,512]{1,0:T(8,128)(2,1)S(1)} %multiply_convert_fusion), channel_id=1, source_target_pairs={{0,64},{64,128},{128,192},{192,256},{256,320},{320,384},{384,448},... | collective-permute-start | bytes 540680 | tf_op jit(solution)/shard_map/ppermute | solution.py:130
  137.2 38.6 %copy-start.4 = (pred[512,512]{0,1:T(8,128)(4,1)}, pred[512,512]{0,1:T(8,128)(4,1)S(1)}, u32[]{:S(2)}) copy-start(pred[512,512]{0,1:T(8,128)(4,1)S(1)} %iota_compare_fusion) | copy-start | bytes 786436
  141.6 7.8 %collective-permute-start.1 = (bf16[176,512]{1,0:T(8,128)(2,1)S(1)}, bf16[176,512]{1,0:T(8,128)(2,1)S(1)}, u32[]{:S(2)}, u32[]{:S(2)}) collective-permute-start(bf16[176,512]{1,0:T(8,128)(2,1)S(1)} %collective-permute-done), channel_id=1, source_target_pairs={{0,64},{64,128},{128,192},{192,256},{256,320},{320,384},{384,448},... | collective-permute-start | bytes 540680 | tf_op jit(solution)/shard_map/ppermute | solution.py:130
  144.2 11.9 %collective-permute-start.4 = (bf16[176,512]{1,0:T(8,128)(2,1)S(1)}, bf16[176,512]{1,0:T(8,128)(2,1)S(1)}, u32[]{:S(2)}, u32[]{:S(2)}) collective-permute-start(bf16[176,512]{1,0:T(8,128)(2,1)S(1)} %multiply_convert_fusion), channel_id=1, source_target_pairs={{0,448},{64,0},{128,64},{192,128},{256,192},{320,256},{384,320},{4... | collective-permute-start | bytes 540680 | tf_op jit(solution)/shard_map/ppermute | solution.py:133
  149.5 11.2 %collective-permute-start.2 = (bf16[176,512]{1,0:T(8,128)(2,1)S(1)}, bf16[176,512]{1,0:T(8,128)(2,1)}, u32[]{:S(2)}, u32[]{:S(2)}) collective-permute-start(bf16[176,512]{1,0:T(8,128)(2,1)S(1)} %collective-permute-done.1), channel_id=1, source_target_pairs={{0,64},{64,128},{128,192},{192,256},{256,320},{320,384},{384,448},... | collective-permute-start | bytes 540680 | tf_op jit(solution)/shard_map/ppermute | solution.py:130
  156.1 7.0 %collective-permute-start.5 = (bf16[176,512]{1,0:T(8,128)(2,1)S(1)}, bf16[176,512]{1,0:T(8,128)(2,1)S(1)}, u32[]{:S(2)}, u32[]{:S(2)}) collective-permute-start(bf16[176,512]{1,0:T(8,128)(2,1)S(1)} %collective-permute-done.4), channel_id=1, source_target_pairs={{0,448},{64,0},{128,64},{192,128},{256,192},{320,256},{384,320},{4... | collective-permute-start | bytes 540680 | tf_op jit(solution)/shard_map/ppermute | solution.py:133
  160.7 8.1 %collective-permute-start.3 = (bf16[176,512]{1,0:T(8,128)(2,1)}, bf16[176,512]{1,0:T(8,128)(2,1)}, u32[]{:S(2)}, u32[]{:S(2)}) collective-permute-start(bf16[176,512]{1,0:T(8,128)(2,1)} %collective-permute-done.2), channel_id=1, source_target_pairs={{0,64},{64,128},{128,192},{192,256},{256,320},{320,384},{384,448},... | collective-permute-start | bytes 540680 | tf_op jit(solution)/shard_map/ppermute | solution.py:130
  163.1 7.8 %collective-permute-start.6 = (bf16[176,512]{1,0:T(8,128)(2,1)S(1)}, bf16[176,512]{1,0:T(8,128)(2,1)S(1)}, u32[]{:S(2)}, u32[]{:S(2)}) collective-permute-start(bf16[176,512]{1,0:T(8,128)(2,1)S(1)} %collective-permute-done.5), channel_id=1, source_target_pairs={{0,448},{64,0},{128,64},{192,128},{256,192},{320,256},{384,320},{4... | collective-permute-start | bytes 540680 | tf_op jit(solution)/shard_map/ppermute | solution.py:133
  169.7 3.4 %copy-start.10 = (bf16[3,176,1408]{2,1,0:T(8,128)(2,1)S(1)}, bf16[3,176,1408]{2,1,0:T(8,128)(2,1)}, u32[]{:S(2)}) copy-start(bf16[3,176,1408]{2,1,0:T(8,128)(2,1)} %param.16) | copy-start | bytes 4460548
  174.2 1.0 copy-start.6
  175.2 51.3 %copy-start.8 = (bf16[2,44,512]{2,1,0:T(8,128)(2,1)}, bf16[2,44,512]{2,1,0:T(8,128)(2,1)S(1)}, u32[]{:S(2)}) copy-start(bf16[2,44,512]{2,1,0:T(8,128)(2,1)S(1)} %get-tuple-element.46) | copy-start | bytes 270340
  175.8 1.4 copy-start.1
  249.6 4.9 %copy-start.2 = (f32[2,512,512]{1,2,0:T(8,128)S(1)}, f32[2,512,512]{1,2,0:T(8,128)}, u32[]{:S(2)}) copy-start(f32[2,512,512]{1,2,0:T(8,128)} %copy-done.1) | copy-start | bytes 6291460
  249.6 4.9 %copy-start.5 = (pred[512,512]{0,1:T(8,128)(4,1)S(1)}, pred[512,512]{0,1:T(8,128)(4,1)}, u32[]{:S(2)}) copy-start(pred[512,512]{0,1:T(8,128)(4,1)} %copy-done.4) | copy-start | bytes 786436
  249.6 4.9 %copy-start.7 = (bf16[1,176,512]{2,1,0:T(8,128)(2,1)S(1)}, bf16[1,176,512]{2,1,0:T(8,128)(2,1)}, u32[]{:S(2)}) copy-start(bf16[1,176,512]{2,1,0:T(8,128)(2,1)} %copy-done.6) | copy-start | bytes 540676
  254.5 1.5 copy-start.3
Sparse Core Ops, SparseCore 0:
  44.1 36.3 reduce-scatter.3
